TPU v7x, 32 devices: a whole 2x2x4 slice. The times are simulated.
32 devices in a mesh: ctx: 16 (over z, y, x), tp: 2 (over core).
Axes of the slice: x: 2, y: 2, z: 4, core: 2. Of those that a mesh axis runs over, the one named last changes fastest.
Arguments:
- ssm_input: bfloat16 [2048, 8192], P('ctx', 'tp'), may hold values from -40 to 40
- ssm_gate: bfloat16 [2048, 8192], P('ctx', 'tp'), may hold values from -4 to 4
- state_write: bfloat16 [2048, 128], P('ctx'), may hold values from -0.5 to 0.5
- state_read: bfloat16 [2048, 128], P('ctx'), may hold values from -0.5 to 0.5
- log_decay: float32 [2048, 32], P('ctx', 'tp'), may hold values from -4 to 0
- skip_gain: float32 [32], P('tp'), may hold values from 0.5 to 1.5
- norm_gain: float32 [8192], P('tp'), may hold values from 0.1 to 1.9
- ssm_cotangent: bfloat16 [2048, 8192], P('ctx', 'tp'), may hold values from -6 to 6
- queries: bfloat16 [2048, 8192], P('ctx', 'tp'), may hold values from -5 to 5
- key_states: bfloat16 [2048, 1024], P('ctx', 'tp'), may hold values from -5 to 5
- value_states: bfloat16 [2048, 1024], P('ctx', 'tp'), may hold values from -6 to 6
- attn_cotangent: bfloat16 [2048, 8192], P('ctx', 'tp'), may hold values from -6 to 6
Outputs:
- ssm_output: bfloat16 [2048, 8192], P('ctx', 'tp')
- input_grad: bfloat16 [2048, 8192], P('ctx', 'tp')
- gate_grad: bfloat16 [2048, 8192], P('ctx', 'tp')
- write_grad: float32 [2048, 128], P('ctx')
- read_grad: float32 [2048, 128], P('ctx')
- attn_output: bfloat16 [2048, 8192], P('ctx', 'tp')
- query_grad: bfloat16 [2048, 8192], P('ctx', 'tp')
- key_grad: bfloat16 [2048, 1024], P('ctx', 'tp')
- value_grad: bfloat16 [2048, 1024], P('ctx', 'tp')
All inputs are finite; a program needn't handle non-finite values.
Results may differ from a plain program's by a relative error of at most 0.035.
Values may be sent and summed in bfloat16 or wider, within the bound.
A program may use at most 192 MiB of HBM per device.

v0:
```python
import jax
import jax.numpy as jnp
from jax import lax
from jax.sharding import PartitionSpec as P

HD = 128
CH = 8192
PRECISE = lax.Precision.HIGHEST
NEGATIVE = -1e30
EPSILON = 1e-05
TILE_KEYS = 1024


def carried_in(x, axis, join, neutral, backward):
    count = lax.axis_size(axis)
    place = lax.axis_index(axis)
    ahead = count - 1 - place if backward else place
    gathered = jax.tree.map(
        lambda a, kind: lax.all_gather(a.astype(kind), axis),
        x,
        jax.tree.map(lambda a: jnp.bfloat16 if a.dtype == jnp.float32 else a.dtype, x),
    )
    state = jax.tree.map(lambda a, e: jnp.zeros_like(a) + jnp.asarray(e, a.dtype), x, neutral)

    def one(turn, state):
        source = count - 1 - turn if backward else turn
        return join(
            state,
            jax.tree.map(
                lambda a, own: lax.dynamic_index_in_dim(a, source, 0, False).astype(own.dtype),
                gathered,
                x,
            ),
        )

    return lax.fori_loop(0, ahead, one, state)


def for_sending(x):

    def short(part):
        return part.astype(jnp.bfloat16) if part.dtype == jnp.float32 else part

    return jax.tree.map(short, x)


def spread(value, axis, source):
    kept = jnp.where(lax.axis_index(axis) == source, value, 0).astype(value.dtype)
    return lax.psum(kept, axis)


def combine(earlier, latter):
    return (earlier[0] * latter[0], latter[0][:, None, None] * earlier[1] + latter[1])


def carried(leading, trailing):
    neutral = (jnp.ones_like(leading[0]), jnp.zeros_like(leading[1]))
    before_state = carried_in(leading, "ctx", combine, neutral, False)
    through = combine(before_state, leading)
    total_state = spread(for_sending(through[1]), "ctx", lax.axis_size("ctx") - 1)
    after_state = carried_in(trailing, "ctx", combine, neutral, True)
    entering = after_state[0][:, None, None] * total_state + after_state[1]
    return (before_state[1], entering)


def ssm_layer(
    ssm_input, ssm_gate, state_write, state_read, log_decay, skip_gain, norm_gain, ssm_cotangent
):
    tok_rows, channel_count = ssm_input.shape
    head_count = log_decay.shape[1]
    half_rows = tok_rows // 2
    head_dim = channel_count // head_count
    input_f32 = ssm_input.astype(jnp.float32).reshape(2, half_rows, head_count, head_dim)
    write_pair = state_write.reshape(2, half_rows, -1)
    read_pair = state_read.reshape(2, half_rows, -1)
    write_f32 = write_pair.astype(jnp.float32)
    read_f32 = read_pair.astype(jnp.float32)
    log_total = jnp.cumsum(log_decay.reshape(2, half_rows, head_count), axis=1)
    by_head = jnp.transpose(log_total, (0, 2, 1))
    log_gap = by_head[:, :, :, None] - by_head[:, :, None, :]
    causal = lax.broadcasted_iota(jnp.int32, (half_rows, half_rows), 0) >= lax.broadcasted_iota(
        jnp.int32, (half_rows, half_rows), 1
    )
    decay = jnp.exp(jnp.where(causal, log_gap, NEGATIVE))
    read_write = jnp.einsum(
        "ctn,csn->cts", read_pair, write_pair, preferred_element_type=jnp.float32
    )
    weights = decay * read_write[:, None, :, :]
    grow_in = jnp.exp(log_total)
    log_last = log_total[:, -1, :]
    shrink = jnp.exp(log_last[:, None, :] - log_total)
    block_decay = jnp.exp(log_last)
    local_state = jnp.einsum(
        "cshp,csn->chpn", input_f32 * shrink[..., None], write_f32, precision=PRECISE
    )
    first_in, second_in = carried(
        (block_decay[0], local_state[0]), (block_decay[1], local_state[1])
    )
    state_in = jnp.stack([first_in, second_in])
    mixed = jnp.einsum("chts,cshp->cthp", weights, input_f32, precision=PRECISE)
    mixed = mixed + grow_in[..., None] * jnp.einsum(
        "chpn,ctn->cthp", state_in, read_f32, precision=PRECISE
    )
    mixed = mixed + skip_gain[None, None, :, None] * input_f32
    mixed = mixed.reshape(tok_rows, channel_count)
    gate_f32 = ssm_gate.astype(jnp.float32)
    sigmoid_gate = jax.nn.sigmoid(gate_f32)
    gated = mixed * gate_f32 * sigmoid_gate
    square_sum = lax.psum(jnp.sum(gated * gated, axis=1), "tp")
    root_mean = jnp.sqrt(square_sum / CH + EPSILON)[:, None]
    normed = gated / root_mean
    ssm_output = (normed * norm_gain).astype(jnp.bfloat16)
    d_normed = ssm_cotangent.astype(jnp.float32) * norm_gain
    inner_sum = lax.psum(jnp.sum(d_normed * normed, axis=1), "tp")
    d_gated = (d_normed - normed * (inner_sum / CH)[:, None]) / root_mean
    d_mixed_flat = d_gated * gate_f32 * sigmoid_gate
    gate_grad = (d_gated * mixed * sigmoid_gate * (1.0 + gate_f32 * (1.0 - sigmoid_gate))).astype(
        jnp.bfloat16
    )
    d_mixed = d_mixed_flat.reshape(2, half_rows, head_count, head_dim)
    local_adjoint = jnp.einsum(
        "cshp,csn->chpn", d_mixed * grow_in[..., None], read_f32, precision=PRECISE
    )
    second_back, first_back = carried(
        (block_decay[1], local_adjoint[1]), (block_decay[0], local_adjoint[0])
    )
    adjoint_in = jnp.stack([first_back, second_back])
    input_g = jnp.einsum("chst,cshp->cthp", weights, d_mixed, precision=PRECISE)
    input_g = input_g + shrink[..., None] * jnp.einsum(
        "chpn,ctn->cthp", adjoint_in, write_f32, precision=PRECISE
    )
    input_g = input_g + skip_gain[None, None, :, None] * d_mixed
    input_grad = input_g.reshape(tok_rows, channel_count).astype(jnp.bfloat16)
    dot_pairs = jnp.einsum("cthp,cshp->chts", d_mixed, input_f32, precision=PRECISE)
    kernel = jnp.sum(decay * dot_pairs, axis=1)
    read_g = jnp.einsum("cts,csn->ctn", kernel, write_f32, precision=PRECISE)
    read_g = read_g + jnp.einsum(
        "cthp,chpn->ctn", d_mixed * grow_in[..., None], state_in, precision=PRECISE
    )
    write_g = jnp.einsum("cst,csn->ctn", kernel, read_f32, precision=PRECISE)
    write_g = write_g + jnp.einsum(
        "cthp,chpn->ctn", input_f32 * shrink[..., None], adjoint_in, precision=PRECISE
    )
    write_grad, read_grad = (
        lax.psum(write_g.reshape(tok_rows, -1).astype(jnp.bfloat16), "tp").astype(jnp.float32),
        lax.psum(read_g.reshape(tok_rows, -1).astype(jnp.bfloat16), "tp").astype(jnp.float32),
    )
    return (ssm_output, input_grad, gate_grad, write_grad, read_grad)


def pick_half(values, half_id):
    return lax.dynamic_index_in_dim(values, half_id, 0, keepdims=False)


def take_half(tree, half_id):
    return jax.tree.map(lambda values: pick_half(values, half_id), tree)


def put_half(tree, half_id, update_tree):
    return jax.tree.map(
        lambda values, replacement: lax.dynamic_update_index_in_dim(
            values, replacement, half_id, 0
        ),
        tree,
        update_tree,
    )


def add_rows(totals, update_rows, row_start):
    current = lax.dynamic_slice_in_dim(totals, row_start, update_rows.shape[0], 0)
    return lax.dynamic_update_slice_in_dim(totals, current + update_rows, row_start, 0)


def score_block(query_block, key_block, key_mask, score_scale):
    raw_scores = (
        jnp.einsum("tkgd,skd->kgts", query_block, key_block, preferred_element_type=jnp.float32)
        * score_scale
    )
    return jnp.where(key_mask, raw_scores, NEGATIVE)


def absorb(soft_state, query_block, key_block, value_block, key_mask, score_scale):
    row_max, weight_sum, accum_out = soft_state
    scores = score_block(query_block, key_block, key_mask, score_scale)
    new_max = jnp.maximum(row_max, jnp.max(scores, axis=-1))
    rescale = jnp.exp(row_max - new_max)
    prob_full = jnp.exp(scores - new_max[..., None])
    accum_out = accum_out * rescale[..., None] + jnp.einsum(
        "kgts,skd->kgtd",
        prob_full.astype(jnp.bfloat16),
        value_block,
        preferred_element_type=jnp.float32,
    )
    return (new_max, weight_sum * rescale + jnp.sum(prob_full, axis=-1), accum_out)


def grad_block(
    query_block, key_block, value_block, cot_block, norm_block, delta_block, key_mask, score_scale
):
    scores = score_block(query_block, key_block, key_mask, score_scale)
    prob_full = jnp.exp(scores - norm_block[..., None])
    weights = prob_full.astype(jnp.bfloat16)
    d_prob = jnp.einsum(
        "tkgd,skd->kgts", cot_block, value_block, preferred_element_type=jnp.float32
    )
    d_score = (prob_full * (d_prob - delta_block[..., None]) * score_scale).astype(jnp.bfloat16)
    query_g = jnp.einsum("kgts,skd->tkgd", d_score, key_block, preferred_element_type=jnp.float32)
    key_g = jnp.einsum("kgts,tkgd->skd", d_score, query_block, preferred_element_type=jnp.float32)
    value_g = jnp.einsum("kgts,tkgd->skd", weights, cot_block, preferred_element_type=jnp.float32)
    return (query_g, key_g, value_g)


def key_positions(first_row, row_count, tok_rows, half_rows, ctx_count):
    row_id = first_row + lax.iota(jnp.int32, row_count)
    device_id = row_id // tok_rows
    local_id = row_id % tok_rows
    block_id = jnp.where(local_id < half_rows, device_id, 2 * ctx_count - 1 - device_id)
    return block_id * half_rows + local_id % half_rows


def over_pieces(by_rows, carry, pieces, tok_rows):
    row_count = pieces[0].shape[0]
    shards = row_count // tok_rows
    group = 1
    for candidate in range(1, shards + 1):
        if shards % candidate == 0 and candidate * tok_rows <= TILE_KEYS:
            group = candidate
    tile_rows = group * tok_rows

    def tile_turn(offset, inner_carry):
        key_rows = lax.dynamic_slice_in_dim(pieces[0], offset * tile_rows, tile_rows, 0)
        value_rows = lax.dynamic_slice_in_dim(pieces[1], offset * tile_rows, tile_rows, 0)
        return by_rows(inner_carry, key_rows, value_rows, offset * tile_rows)

    return lax.fori_loop(0, shards // group, tile_turn, carry)


def attention(queries, key_states, value_states, attn_cotangent):
    tok_rows = queries.shape[0]
    half_rows = tok_rows // 2
    kv_count = key_states.shape[1] // HD
    group_size = queries.shape[1] // HD // kv_count
    score_scale = HD ** (-0.5)
    ctx_count = lax.axis_size("ctx")
    own_index = lax.axis_index("ctx")
    query_pair = queries.reshape(2, half_rows, kv_count, group_size, HD)
    cot_pair = attn_cotangent.reshape(2, half_rows, kv_count, group_size, HD)
    block_starts = jnp.stack([own_index, 2 * ctx_count - 1 - own_index]) * half_rows
    query_pos = block_starts[:, None] + lax.iota(jnp.int32, half_rows)[None, :]

    def forward_rows(soft_state, key_rows, value_rows, first_row):
        row_count = key_rows.shape[0]
        key_pos = key_positions(first_row, row_count, tok_rows, half_rows, ctx_count)
        key_block = key_rows.reshape(row_count, kv_count, HD)
        value_block = value_rows.reshape(row_count, kv_count, HD)
        for half_id in range(2):
            key_mask = key_pos[None, :] <= query_pos[half_id][:, None]
            soft_state = put_half(
                soft_state,
                half_id,
                absorb(
                    take_half(soft_state, half_id),
                    query_pair[half_id],
                    key_block,
                    value_block,
                    key_mask,
                    score_scale,
                ),
            )
        return soft_state

    start_state = (
        jnp.full((2, kv_count, group_size, half_rows), NEGATIVE, jnp.float32),
        jnp.zeros((2, kv_count, group_size, half_rows), jnp.float32),
        jnp.zeros((2, kv_count, group_size, half_rows, HD), jnp.float32),
    )
    row_max, weight_sum, accum_out = over_pieces(
        forward_rows,
        start_state,
        (
            lax.all_gather(key_states, "ctx", axis=0, tiled=True),
            lax.all_gather(value_states, "ctx", axis=0, tiled=True),
        ),
        tok_rows,
    )
    out_pair = jnp.transpose(accum_out / weight_sum[..., None], (0, 3, 1, 2, 4))
    attn_output = out_pair.reshape(tok_rows, -1).astype(jnp.bfloat16)
    norm_pair = row_max + jnp.log(weight_sum)
    delta_rows = jnp.sum(
        attn_output.reshape(2, half_rows, kv_count, group_size, HD).astype(jnp.float32)
        * cot_pair.astype(jnp.float32),
        axis=-1,
    )
    delta_pair = jnp.transpose(delta_rows, (0, 2, 3, 1))

    def backward_rows(carry, key_rows, value_rows, first_row):
        row_count = key_rows.shape[0]
        key_pos = key_positions(first_row, row_count, tok_rows, half_rows, ctx_count)
        key_block = key_rows.reshape(row_count, kv_count, HD)
        value_block = value_rows.reshape(row_count, kv_count, HD)
        dq_pair, dk_all, dv_all = carry
        for half_id in range(2):
            key_mask = key_pos[None, :] <= query_pos[half_id][:, None]
            block_grads = grad_block(
                query_pair[half_id],
                key_block,
                value_block,
                cot_pair[half_id],
                norm_pair[half_id],
                delta_pair[half_id],
                key_mask,
                score_scale,
            )
            dq_pair = dq_pair.at[half_id].add(block_grads[0])
            dk_all = add_rows(dk_all, block_grads[1], first_row)
            dv_all = add_rows(dv_all, block_grads[2], first_row)
        return (dq_pair, dk_all, dv_all)

    all_rows = tok_rows * ctx_count
    grad_start = (
        jnp.zeros((2, half_rows, kv_count, group_size, HD), jnp.float32),
        jnp.zeros((all_rows, kv_count, HD), jnp.float32),
        jnp.zeros((all_rows, kv_count, HD), jnp.float32),
    )
    dq_pair, dk_all, dv_all = over_pieces(
        backward_rows,
        grad_start,
        (
            lax.all_gather(key_states, "ctx", axis=0, tiled=True),
            lax.all_gather(value_states, "ctx", axis=0, tiled=True),
        ),
        tok_rows,
    )
    dk_mine, dv_mine = (
        lax.psum_scatter(
            dk_all.astype(jnp.bfloat16), "ctx", scatter_dimension=0, tiled=True
        ).astype(jnp.float32),
        lax.psum_scatter(
            dv_all.astype(jnp.bfloat16), "ctx", scatter_dimension=0, tiled=True
        ).astype(jnp.float32),
    )
    query_grad = dq_pair.reshape(tok_rows, -1).astype(jnp.bfloat16)
    key_grad = dk_mine.reshape(tok_rows, -1).astype(jnp.bfloat16)
    value_grad = dv_mine.reshape(tok_rows, -1).astype(jnp.bfloat16)
    return (attn_output, query_grad, key_grad, value_grad)


def per_device(
    ssm_input,
    ssm_gate,
    state_write,
    state_read,
    log_decay,
    skip_gain,
    norm_gain,
    ssm_cotangent,
    queries,
    key_states,
    value_states,
    attn_cotangent,
):
    ssm_results = ssm_layer(
        ssm_input, ssm_gate, state_write, state_read, log_decay, skip_gain, norm_gain, ssm_cotangent
    )
    attn_results = attention(queries, key_states, value_states, attn_cotangent)
    return ssm_results + attn_results


def solution(mesh):
    placed = (
        P("ctx", "tp"),
        P("ctx", "tp"),
        P("ctx", None),
        P("ctx", None),
        P("ctx", "tp"),
        P("tp"),
        P("tp"),
        P("ctx", "tp"),
        P("ctx", "tp"),
        P("ctx", "tp"),
        P("ctx", "tp"),
        P("ctx", "tp"),
    )
    return jax.shard_map(
        per_device,
        mesh=mesh,
        in_specs=placed,
        out_specs=(
            P("ctx", "tp"),
            P("ctx", "tp"),
            P("ctx", "tp"),
            P("ctx", None),
            P("ctx", None),
            P("ctx", "tp"),
            P("ctx", "tp"),
            P("ctx", "tp"),
            P("ctx", "tp"),
        ),
        check_vma=False,
    )
```

profile of v0, /device:TPU:0, one launch (start us, length us, event | category | flops | bytes accessed | tf_op | source)
XLA Modules:
  0.0 1338.4 jit_solution(10396937734925266200)
XLA Ops:
  13.3 3.8 fusion.126
  21.1 42.3 %all-gather = bf16[16,1,16]{2,1,0:T(2,128)(2,1)S(1)} all-gather(bf16[1,1,16]{2,1,0:T(2,128)(2,1)S(1)} %get-tuple-element.1035), channel_id=1, replica_groups=mesh['ctx'=16,'tp'=2] {'ctx'}, dimensions={0}, use_global_device_ids=true | all-gather | bytes 544 | tf_op jit(solution)/shard_map/all_gather | solution.py:19
  68.1 9.3 all-gather.17.cloned.1.call-done
  77.4 64.8 %all-gather.19.cloned.1.call-done = bf16[2048,512]{0,1:T(8,128)(2,1)} async-done(((bf16[128,512]{0,1:T(8,128)(2,1)}), bf16[2048,512]{0,1:T(8,128)(2,1)}) %all-gather.19.cloned.1.call-update) | async-done | bytes 2097168 | tf_op jit(solution)/shard_map/all_gather | solution.py:282
  142.4 28.6 %while.98 = (s32[]{:T(128)}, f32[2,4,8,64]{3,2,1,0:T(8,128)S(1)}, f32[2,4,8,64]{3,2,1,0:T(8,128)S(1)}, f32[2,4,8,64,128]{4,3,2,1,0:T(8,128)S(1)}, s32[2,64]{1,0:...) while((s32[]{:T(128)}, f32[2,4,8,64]{3,2,1,0:T(8,128)S(1)}, ...), condition=%wide.region_23.24_spmd, body=%wide.region_18.23_spmd.sunk | while | flops 2194853888 | bytes 69060272 | solution.py:235
  171.8 4.3 multiply_reduce_fusion
  177.8 157.5 %all-gather.9.cloned.1.call-done = bf16[16,16,256,128]{3,2,1,0:T(8,128)(2,1)} async-done(((bf16[1,16,256,128]{3,2,1,0:T(8,128)(2,1)}), bf16[16,16,256,128]{3,2,1,0:T(8,128)(2,1)}) %all-gather.9.cloned.1.call-update) | async-done | bytes 16777232 | tf_op jit(solution)/shard_map/all_gather | solution.py:19
  335.5 3.7 fusion.164
  344.1 65.2 %while.99 = (s32[]{:T(128)}, f32[2,64,4,8,128]{4,1,3,2,0:T(8,128)S(1)}, f32[2048,4,128]{2,0,1:T(8,128)}, f32[2048,4,128]{2,0,1:T(8,128)}, bf16[2048,512]{0,1:T(8...) while((s32[]{:T(128)}, ...), condition=%wide.region_26.27_spmd, body=%wide.region_25.26_spmd.sunk | while | flops 5417635840 | bytes 150054832 | solution.py:235
  363.3 7.4 fusion.328
  370.8 5.9 fusion.329
  395.7 7.5 fusion.328
  403.2 5.9 fusion.329
  409.3 4.0 convert_element_type.295
  414.2 66.9 %all-gather.1 = bf16[16,1,16]{2,1,0:T(2,128)(2,1)S(1)} all-gather(bf16[1,1,16]{2,1,0:T(2,128)(2,1)S(1)} %copy-done.38), channel_id=1, replica_groups=mesh['ctx'=16,'tp'=2] {'ctx'}, dimensions={0}, use_global_device_ids=true | all-gather | bytes 544 | tf_op jit(solution)/shard_map/all_gather | solution.py:19
  484.1 3.8 convert_element_type.297
  488.0 40.5 %all-gather.11.cloned.1.call-done = bf16[16,16,256,128]{3,2,1,0:T(8,128)(2,1)} async-done(((bf16[1,16,256,128]{3,2,1,0:T(8,128)(2,1)}), bf16[16,16,256,128]{3,2,1,0:T(8,128)(2,1)}) %all-gather.11.cloned.1.call-update) | async-done | bytes 16777232 | tf_op jit(solution)/shard_map/all_gather | solution.py:19
  530.1 53.4 %while.95 = (s32[]{:T(128)}, f32[16]{0:T(128)S(1)}, f32[16,256,128]{2,1,0:T(8,128)}, s32[]{:T(128)}, bf16[16,16]{1,0:T(8,128)(2,1)S(1)}, /*index=5*/bf16[16,16,2...) while((s32[]{:T(128)}, f32[16]{0:T(128)S(1)}, f32[16,256,128]{2,1,0:T(8,128)}, ...), condition=%wide.region_4.5_spmd, body=%wide.region_3.4_spmd.sunk | while | flops 1572902 | bytes 5243331 | solution.py:36
  537.1 3.7 convert_add_fusion.9
  547.9 3.5 convert_add_fusion.9
  551.5 3.6 convert_add_fusion.9
  555.1 3.5 convert_add_fusion.9
  562.2 3.5 convert_add_fusion.9
  565.7 3.5 convert_add_fusion.9
  572.8 3.6 convert_add_fusion.9
  583.5 60.7 %all-reduce.5.cloned.1.call-done = bf16[16,256,128]{2,1,0:T(8,128)(2,1)} async-done(((bf16[16,256,128]{2,1,0:T(8,128)(2,1)}), bf16[16,256,128]{2,1,0:T(8,128)(2,1)}) %all-reduce.5.cloned.1.call-update) | async-done | bytes 1048592 | tf_op jit(solution)/shard_map/psum | solution.py:49
  658.1 4.1 multiply_reduce_fusion.1
  664.6 5.2 fusion.135
  671.9 4.4 fusion.144
  683.7 42.3 %reduce-scatter.3.cloned.1.call-done = bf16[128,4,128]{2,0,1:T(8,128)(2,1)} async-done(((bf16[2048,4,128]{2,0,1:T(8,128)(2,1)}), bf16[128,4,128]{2,0,1:T(8,128)(2,1)}) %reduce-scatter.3.cloned.1.call-update) | async-done | bytes 131088 | tf_op jit(solution)/shard_map/reduce_scatter | solution.py:335
  727.5 78.9 %reduce-scatter.5.cloned.1.call-done = bf16[128,4,128]{2,0,1:T(8,128)(2,1)} async-done(((bf16[2048,4,128]{2,0,1:T(8,128)(2,1)}), bf16[128,4,128]{2,0,1:T(8,128)(2,1)}) %reduce-scatter.5.cloned.1.call-update) | async-done | bytes 131088 | tf_op jit(solution)/shard_map/reduce_scatter | solution.py:338
  808.0 6.1 fusion.158
  817.5 4.7 fusion.150
  822.1 175.3 %all-gather.15.cloned.1.call-done = bf16[16,16,256,128]{3,2,1,0:T(8,128)(2,1)} async-done(((bf16[1,16,256,128]{3,2,1,0:T(8,128)(2,1)}), bf16[16,16,256,128]{3,2,1,0:T(8,128)(2,1)}) %all-gather.15.cloned.1.call-update) | async-done | bytes 16777232 | tf_op jit(solution)/shard_map/all_gather | solution.py:19
  1001.4 188.7 %all-gather.13.cloned.1.call-done = bf16[16,16,256,128]{3,2,1,0:T(8,128)(2,1)} async-done(((bf16[1,16,256,128]{3,2,1,0:T(8,128)(2,1)}), bf16[16,16,256,128]{3,2,1,0:T(8,128)(2,1)}) %all-gather.13.cloned.1.call-update) | async-done | bytes 16777232 | tf_op jit(solution)/shard_map/all_gather | solution.py:19
  1191.6 63.5 %while.96 = (s32[]{:T(128)}, f32[16]{0:T(128)S(1)}, f32[16,256,128]{2,1,0:T(8,128)}, s32[]{:T(128)}, bf16[16,16]{1,0:T(8,128)(2,1)}, /*index=5*/bf16[16,16,256,1...) while((s32[]{:T(128)}, f32[16]{0:T(128)S(1)}, f32[16,256,128]{2,1,0:T(8,128)}, ...), condition=%wide.region_11.12_spmd, body=%wide.region_10.11_spmd.sunk | while | flops 1572902 | bytes 5243331 | solution.py:36
  1204.9 3.5 convert_add_fusion.10
  1209.1 3.6 convert_add_fusion.10
  1213.4 3.5 convert_add_fusion.10
  1217.6 3.6 convert_add_fusion.10
  1226.1 3.6 convert_add_fusion.10
  1230.4 3.5 convert_add_fusion.10
  1234.6 3.6 convert_add_fusion.10
  1243.1 3.5 convert_add_fusion.10
  1251.6 3.5 convert_add_fusion.10
  1255.1 50.6 %all-reduce.7.cloned.1.call-done = bf16[16,256,128]{2,1,0:T(8,128)(2,1)} async-done(((bf16[16,256,128]{2,1,0:T(8,128)(2,1)}), bf16[16,256,128]{2,1,0:T(8,128)(2,1)}) %all-reduce.7.cloned.1.call-update) | async-done | bytes 1048592 | tf_op jit(solution)/shard_map/psum | solution.py:49
  1311.9 6.3 fusion.138
  1320.3 8.7 all-reduce.9.cloned.1.call-done
  (285 shorter events, 201.9 us)
Async XLA Ops:
  7.2 474.0 %copy-start = (bf16[128,128]{1,0:T(8,128)(2,1)S(1)}, bf16[128,128]{1,0:T(8,128)(2,1)}, u32[]{:S(2)}) copy-start(bf16[128,128]{1,0:T(8,128)(2,1)} %param.31) | copy-start | bytes 98308
  7.2 5.0 copy-start.36
  7.2 6.1 copy-start.26
  7.2 70.1 %all-gather.17.cloned.1.call-start = ((), (), s32[]{:S(2)}) async-start(), calls=%async_computation.8 | async-start | bytes 2228224 | tf_op jit(solution)/shard_map/all_gather | solution.py:281
  8.9 133.2 %all-gather.19.cloned.1.call-start = ((), (), s32[]{:S(2)}) async-start(), calls=%async_computation.9 | async-start | bytes 2228224 | tf_op jit(solution)/shard_map/all_gather | solution.py:282
  10.7 324.6 %all-gather.9.cloned.1.call-start = ((), (), s32[]{:S(2)}) async-start(), calls=%async_computation.2 | async-start | bytes 17825792 | tf_op jit(solution)/shard_map/all_gather | solution.py:19
  12.2 4.9 copy-start.9
  12.4 4.7 copy-start.24
  13.3 3.8 copy-start.30
  17.1 2.6 copy-start.14
  19.8 43.6 %copy-start.22 = (bf16[128,4096]{1,0:T(8,128)(2,1)S(1)}, bf16[128,4096]{1,0:T(8,128)(2,1)}, u32[]{:S(2)}) copy-start(bf16[128,4096]{1,0:T(8,128)(2,1)} %param.39) | copy-start | bytes 3145732
  19.8 508.7 %all-gather.11.cloned.1.call-start = ((), (), s32[]{:S(2)}) async-start(), calls=%async_computation.3 | async-start | bytes 17825792 | tf_op jit(solution)/shard_map/all_gather | solution.py:19
  20.4 623.8 %all-reduce.5.cloned.1.call-start = ((), (), s32[]{:S(2)}) async-start(), calls=%async_computation.4 | async-start | bytes 2097152 | tf_op jit(solution)/shard_map/psum | solution.py:49
  63.6 2.3 copy-start.16
  335.5 3.8 copy-start.3
  335.5 3.7 copy-start.34
  339.3 386.7 %reduce-scatter.3.cloned.1.call-start = ((), (), s32[]{:S(2)}) async-start(), calls=%async_computation.10 | async-start | bytes 2228224 | tf_op jit(solution)/shard_map/reduce_scatter | solution.py:335
  346.6 2.2 copy-start.23
  348.6 3.3 copy-start.29
  348.6 5.9 copy-start.28
  348.7 3.1 copy-start.21
  348.8 5.8 copy-start.20
  363.3 7.5 copy-start.2
  379.0 2.2 copy-start.23
  381.0 3.3 copy-start.29
  381.0 5.9 copy-start.28
  381.2 3.1 copy-start.21
  381.2 5.8 copy-start.20
  395.7 7.5 copy-start.2
  413.3 67.8 %copy-start.32 = (f32[2,64,16]{2,1,0:T(8,128)S(1)}, f32[2,64,16]{2,1,0:T(8,128)}, u32[]{:S(2)}) copy-start(f32[2,64,16]{2,1,0:T(8,128)} %get-tuple-element.1031) | copy-start | bytes 24580
  413.3 67.9 %copy-start.27 = (bf16[128,128]{1,0:T(8,128)(2,1)S(1)}, bf16[128,128]{1,0:T(8,128)(2,1)}, u32[]{:S(2)}) copy-start(bf16[128,128]{1,0:T(8,128)(2,1)} %param.30) | copy-start | bytes 98308
  413.3 68.0 %copy-start.10 = (bf16[16,8,16,256]{3,2,1,0:T(8,128)(2,1)S(1)}, bf16[16,8,16,256]{3,2,1,0:T(8,128)(2,1)}, u32[]{:S(2)}) copy-start(bf16[16,8,16,256]{3,2,1,0:T(8,128)(2,1)} %copy-done.9) | copy-start | bytes 3145732
  413.3 393.0 %reduce-scatter.5.cloned.1.call-start = ((), (), s32[]{:S(2)}) async-start(), calls=%async_computation.11 | async-start | bytes 2228224 | tf_op jit(solution)/shard_map/reduce_scatter | solution.py:338
  487.9 509.5 %all-gather.15.cloned.1.call-start = ((), (), s32[]{:S(2)}) async-start(), calls=%async_computation.6 | async-start | bytes 17825792 | tf_op jit(solution)/shard_map/all_gather | solution.py:19
  644.2 2.5 copy-start.4
  644.2 3.2 copy-start.18
  644.2 3.2 copy-start.35
  646.5 4.1 copy-start.12
  651.8 3.0 copy-start.17
  653.5 4.6 copy-start.33
  676.3 2.7 copy-start.15
  679.0 511.0 %all-gather.13.cloned.1.call-start = ((), (), s32[]{:S(2)}) async-start(), calls=%async_computation.5 | async-start | bytes 17825792 | tf_op jit(solution)/shard_map/all_gather | solution.py:19
  679.8 625.9 %all-reduce.7.cloned.1.call-start = ((), (), s32[]{:S(2)}) async-start(), calls=%async_computation.7 | async-start | bytes 2097152 | tf_op jit(solution)/shard_map/psum | solution.py:49
  681.7 126.3 %copy-start.5 = (f32[16,256,128]{2,1,0:T(8,128)S(1)}, f32[16,256,128]{2,1,0:T(8,128)}, u32[]{:S(2)}) copy-start(f32[16,256,128]{2,1,0:T(8,128)} %copy-done.3) | copy-start | bytes 6291460
  808.0 6.1 copy-start.7
  808.0 6.1 copy-start.11
  1001.3 327.6 %all-reduce.9.cloned.1.call-start = ((), (), s32[]{:S(2)}) async-start(), calls=%async_computation.12 | async-start | bytes 131072 | tf_op jit(solution)/shard_map/psum | solution.py:145
  1307.9 3.1 copy-start.13
  (9 other events, 13.0 us)
Sparse Core Ops, SparseCore 0:
  11.3 65.9 all-gather.16
  80.6 61.4 all-gather.18
  145.5 189.7 all-gather.8
  338.5 189.9 all-gather.10
  534.2 109.9 all-reduce.4
  646.3 79.6 reduce-scatter.2
  728.2 78.1 reduce-scatter.4
  809.2 188.2 all-gather.14
  1000.2 189.7 all-gather.12
  1195.8 109.9 all-reduce.6
  1312.1 16.8 all-reduce.8
where the time goes:
time: 1350 us; the launch traced here: 1340 us
  waiting for transfers between devices  879 us (65%)
  other arithmetic  165 us (12%)
  blocking collectives  114 us (8%)
  matrix products  110 us (8%)
  local copies, waits for them, and re-layouts  54 us (4%)
  between operations  14.6 us (1%)
    all_gather x4, waiting for transfers between devices, carried_in(): lax.all_gather(a.astype(kind), axis)  562 us
    psum x2, waiting for transfers between devices, spread(): return lax.psum(kept, axis)  111 us
    all_gather x2, blocking collectives, carried_in(): lax.all_gather(a.astype(kind), axis)  109 us
    add x30, other arithmetic, combine(): latter[0][:, None, None] * earlier[1] + latter[1]  106 us
    reduce_scatter x1, waiting for transfers between devices, attention(): lax.psum_scatter(dv_all.astype(jnp.bfloat16), 'ctx', scatter_dimension=0,...  78.9 us
    all_gather x1, waiting for transfers between devices, attention(): lax.all_gather(value_states, 'ctx', axis=0, tiled=True)  64.8 us
    reduce_scatter x1, waiting for transfers between devices, attention(): lax.psum_scatter(dk_all.astype(jnp.bfloat16), 'ctx', scatter_dimension=0,...  42.3 us
  transfers between devices with their start and end apart: 11, of which 11 were waited for; matrix products, arithmetic and copies ran while one was open for 23% of the time, Pallas kernels for 0%

commit v1 on v0

--- a/solution.py
+++ b/solution.py
@@ -46,7 +46,7 @@
 
 def spread(value, axis, source):
     kept = jnp.where(lax.axis_index(axis) == source, value, 0).astype(value.dtype)
-    return lax.psum(kept, axis)
+    return jnp.sum(lax.all_gather(kept, axis), 0)
 
 
 def combine(earlier, latter):

time: 1350 us -> 1520 us (1.13)
  waiting for transfers between devices: 879 us -> 1050 us
    all_gather x0 -> x2, waiting for transfers between devices: none -> 289 us  [spread(): return jnp.sum(lax.all_gather(kept, axis), 0)]
    psum x2 -> x0, waiting for transfers between devices: 111 us -> none  [spread(): return lax.psum(kept, axis)]
    all_gather x4, waiting for transfers between devices: 562 us -> 521 us  [carried_in(): lax.all_gather(a.astype(kind), axis)]
    reduce_scatter x1, waiting for transfers between devices: 42.3 us -> 71.6 us  [attention(): lax.psum_scatter(dk_all.astype(jnp.bfloat16), 'ctx', scatter_dimension=0,...]
    add x30, other arithmetic: 106 us -> 83.8 us  [combine(): latter[0][:, None, None] * earlier[1] + latter[1]]
    reduce_sum x0 -> x2, other arithmetic: none -> 19.8 us  [spread(): return jnp.sum(lax.all_gather(kept, axis), 0)]
  transfers between devices with their start and end apart: 11 -> 11, of which waited for: 11 -> 11; matrix products, arithmetic and copies ran while one was open for 23% -> 19% of each run, Pallas kernels for 0% -> 0%
where the time goes in v1:
time: 1520 us; the launch traced here: 1510 us
  waiting for transfers between devices  1050 us (69%)
  other arithmetic  160 us (11%)
  blocking collectives  116 us (8%)
  matrix products  115 us (8%)
  local copies, waits for them, and re-layouts  45.9 us (3%)
    all_gather x4, waiting for transfers between devices, carried_in(): lax.all_gather(a.astype(kind), axis)  521 us
    all_gather x2, waiting for transfers between devices, spread(): return jnp.sum(lax.all_gather(kept, axis), 0)  289 us
    all_gather x2, blocking collectives, carried_in(): lax.all_gather(a.astype(kind), axis)  110 us
    add x30, other arithmetic, combine(): latter[0][:, None, None] * earlier[1] + latter[1]  83.8 us
    reduce_scatter x1, waiting for transfers between devices, attention(): lax.psum_scatter(dv_all.astype(jnp.bfloat16), 'ctx', scatter_dimension=0,...  78.6 us
    reduce_scatter x1, waiting for transfers between devices, attention(): lax.psum_scatter(dk_all.astype(jnp.bfloat16), 'ctx', scatter_dimension=0,...  71.6 us
    all_gather x1, waiting for transfers between devices, attention(): lax.all_gather(value_states, 'ctx', axis=0, tiled=True)  64.6 us
  transfers between devices with their start and end apart: 11, of which 11 were waited for; matrix products, arithmetic and copies ran while one was open for 19% of the time, Pallas kernels for 0%

profile of v1, /device:TPU:0, one launch (start us, length us, event | category | flops | bytes accessed | tf_op | source)
XLA Modules:
  0.0 1506.8 jit_solution(10608342710527289555)
XLA Ops:
  9.1 3.8 fusion.126
  16.4 42.5 %all-gather.2 = bf16[16,1,16]{2,1,0:T(2,128)(2,1)S(1)} all-gather(bf16[1,1,16]{2,1,0:T(2,128)(2,1)S(1)} %get-tuple-element.1035), channel_id=1, replica_groups=mesh['ctx'=16,'tp'=2] {'ctx'}, dimensions={0}, use_global_device_ids=true | all-gather | bytes 544 | tf_op jit(solution)/shard_map/all_gather | solution.py:19
  59.4 150.6 %all-gather.13.cloned.1.call-done = bf16[16,16,256,128]{3,2,1,0:T(8,128)(2,1)} async-done(((bf16[1,16,256,128]{3,2,1,0:T(8,128)(2,1)}), bf16[16,16,256,128]{3,2,1,0:T(8,128)(2,1)}) %all-gather.13.cloned.1.call-update) | async-done | bytes 16777232 | tf_op jit(solution)/shard_map/all_gather | solution.py:19
  210.3 3.7 fusion.164
  216.8 68.0 %all-gather.3 = bf16[16,1,16]{2,1,0:T(2,128)(2,1)S(1)} all-gather(bf16[1,1,16]{2,1,0:T(2,128)(2,1)S(1)} %get-tuple-element.1036), channel_id=1, replica_groups=mesh['ctx'=16,'tp'=2] {'ctx'}, dimensions={0}, use_global_device_ids=true | all-gather | bytes 544 | tf_op jit(solution)/shard_map/all_gather | solution.py:19
  288.4 115.0 %all-gather.15.cloned.1.call-done = bf16[16,16,256,128]{3,2,1,0:T(8,128)(2,1)} async-done(((bf16[1,16,256,128]{3,2,1,0:T(8,128)(2,1)}), bf16[16,16,256,128]{3,2,1,0:T(8,128)(2,1)}) %all-gather.15.cloned.1.call-update) | async-done | bytes 16777232 | tf_op jit(solution)/shard_map/all_gather | solution.py:19
  405.0 55.1 %while.95 = (s32[]{:T(128)}, f32[16]{0:T(128)S(1)}, f32[16,256,128]{2,1,0:T(8,128)}, s32[]{:T(128)}, bf16[16,16]{1,0:T(8,128)(2,1)S(1)}, /*index=5*/bf16[16,16,2...) while((s32[]{:T(128)}, f32[16]{0:T(128)S(1)}, f32[16,256,128]{2,1,0:T(8,128)}, ...), condition=%wide.region_4.5_spmd, body=%wide.region_3.4_spmd.sunk | while | flops 1572902 | bytes 5243331 | solution.py:36
  405.0 3.6 convert_add_fusion.9
  412.1 4.0 convert_add_fusion.9
  419.7 3.6 convert_add_fusion.9
  423.3 3.6 convert_add_fusion.9
  426.8 3.6 convert_add_fusion.9
  430.4 3.6 convert_add_fusion.9
  434.0 3.6 convert_add_fusion.9
  444.7 4.4 convert_add_fusion.9
  452.7 3.6 convert_add_fusion.9
  456.3 3.6 convert_add_fusion.9
  460.1 136.5 %all-gather.25.cloned.1.call-done = bf16[256,256,128]{2,1,0:T(8,128)(2,1)} async-done(((bf16[16,256,128]{2,1,0:T(8,128)(2,1)}), bf16[256,256,128]{2,1,0:T(8,128)(2,1)}) %all-gather.25.cloned.1.call-update) | async-done | bytes 16777232 | tf_op jit(solution)/shard_map/all_gather | solution.py:49
  596.6 9.9 reduce_sum.98
  624.5 4.6 fusion.135
  631.1 4.4 fusion.144
  641.7 19.5 %all-gather.21.cloned.1.call-done = bf16[2048,512]{0,1:T(8,128)(2,1)} async-done(((bf16[128,512]{0,1:T(8,128)(2,1)}), bf16[2048,512]{0,1:T(8,128)(2,1)}) %all-gather.21.cloned.1.call-update) | async-done | bytes 2097168 | tf_op jit(solution)/shard_map/all_gather | solution.py:281
  661.2 64.6 %all-gather.23.cloned.1.call-done = bf16[2048,512]{0,1:T(8,128)(2,1)} async-done(((bf16[128,512]{0,1:T(8,128)(2,1)}), bf16[2048,512]{0,1:T(8,128)(2,1)}) %all-gather.23.cloned.1.call-update) | async-done | bytes 2097168 | tf_op jit(solution)/shard_map/all_gather | solution.py:282
  726.1 28.6 %while.98 = (s32[]{:T(128)}, f32[2,4,8,64]{3,2,1,0:T(8,128)S(1)}, f32[2,4,8,64]{3,2,1,0:T(8,128)S(1)}, f32[2,4,8,64,128]{4,3,2,1,0:T(8,128)S(1)}, s32[2,64]{1,0:...) while((s32[]{:T(128)}, f32[2,4,8,64]{3,2,1,0:T(8,128)S(1)}, ...), condition=%wide.region_23.24_spmd, body=%wide.region_18.23_spmd.sunk | while | flops 2194853888 | bytes 69060272 | solution.py:235
  755.5 4.3 multiply_reduce_fusion
  765.7 66.2 %while.99 = (s32[]{:T(128)}, f32[2,64,4,8,128]{4,1,3,2,0:T(8,128)S(1)}, f32[2048,4,128]{2,0,1:T(8,128)}, f32[2048,4,128]{2,0,1:T(8,128)}, bf16[2048,512]{0,1:T(8...) while((s32[]{:T(128)}, ...), condition=%wide.region_26.27_spmd, body=%wide.region_25.26_spmd.sunk | while | flops 5417635840 | bytes 115910384 | solution.py:235
  779.2 4.5 fusion.326
  783.8 4.5 fusion.327
  788.3 5.2 fusion.328
  793.5 5.2 fusion.329
  812.0 4.5 fusion.326
  816.5 4.5 fusion.327
  821.1 5.2 fusion.328
  826.3 5.2 fusion.329
  831.9 3.8 convert_element_type.299
  835.8 3.8 convert_element_type.301
  840.4 78.5 %all-gather.19.cloned.1.call-done = bf16[16,16,256,128]{3,2,1,0:T(8,128)(2,1)} async-done(((bf16[1,16,256,128]{3,2,1,0:T(8,128)(2,1)}), bf16[16,16,256,128]{3,2,1,0:T(8,128)(2,1)}) %all-gather.19.cloned.1.call-update) | async-done | bytes 16777232 | tf_op jit(solution)/shard_map/all_gather | solution.py:19
  921.1 3.7 fusion.165
  928.3 71.6 %reduce-scatter.3.cloned.1.call-done = bf16[128,4,128]{2,0,1:T(8,128)(2,1)} async-done(((bf16[2048,4,128]{2,0,1:T(8,128)(2,1)}), bf16[128,4,128]{2,0,1:T(8,128)(2,1)}) %reduce-scatter.3.cloned.1.call-update) | async-done | bytes 131088 | tf_op jit(solution)/shard_map/reduce_scatter | solution.py:335
  1001.5 78.6 %reduce-scatter.5.cloned.1.call-done = bf16[128,4,128]{2,0,1:T(8,128)(2,1)} async-done(((bf16[2048,4,128]{2,0,1:T(8,128)(2,1)}), bf16[128,4,128]{2,0,1:T(8,128)(2,1)}) %reduce-scatter.5.cloned.1.call-update) | async-done | bytes 131088 | tf_op jit(solution)/shard_map/reduce_scatter | solution.py:338
  1081.6 6.1 fusion.158
  1091.2 4.7 fusion.150
  1095.9 176.4 %all-gather.17.cloned.1.call-done = bf16[16,16,256,128]{3,2,1,0:T(8,128)(2,1)} async-done(((bf16[1,16,256,128]{3,2,1,0:T(8,128)(2,1)}), bf16[16,16,256,128]{3,2,1,0:T(8,128)(2,1)}) %all-gather.17.cloned.1.call-update) | async-done | bytes 16777232 | tf_op jit(solution)/shard_map/all_gather | solution.py:19
  1272.5 40.1 %while.96 = (s32[]{:T(128)}, f32[16]{0:T(128)S(1)}, f32[16,256,128]{2,1,0:T(8,128)S(1)}, s32[]{:T(128)}, bf16[16,16]{1,0:T(8,128)(2,1)}, /*index=5*/bf16[16,16,2...) while((s32[]{:T(128)}, f32[16]{0:T(128)S(1)}, f32[16,256,128]{2,1,0:T(8,128)S(1)}, ...), condition=%wide.region_11.12_spmd, body=%wide.region_10.11_spmd.sunk | while | flops 1572902 | bytes 5243331 | solution.py:36
  1312.7 152.1 %all-gather.27.cloned.1.call-done = bf16[256,256,128]{2,1,0:T(8,128)(2,1)} async-done(((bf16[16,256,128]{2,1,0:T(8,128)(2,1)}), bf16[256,256,128]{2,1,0:T(8,128)(2,1)}) %all-gather.27.cloned.1.call-update) | async-done | bytes 16777232 | tf_op jit(solution)/shard_map/all_gather | solution.py:49
  1464.8 9.9 reduce_sum.101
  1481.2 6.3 fusion.138
  1489.6 7.8 all-reduce.3.cloned.1.call-done
  (277 shorter events, 183.5 us)
Async XLA Ops:
  7.2 277.7 %copy-start = (bf16[128,128]{1,0:T(8,128)(2,1)S(1)}, bf16[128,128]{1,0:T(8,128)(2,1)}, u32[]{:S(2)}) copy-start(bf16[128,128]{1,0:T(8,128)(2,1)} %param.31) | copy-start | bytes 98308
  7.2 1.6 copy-start.38
  7.2 1.9 copy-start.22
  7.2 202.9 %all-gather.13.cloned.1.call-start = ((), (), s32[]{:S(2)}) async-start(), calls=%async_computation.2 | async-start | bytes 17825792 | tf_op jit(solution)/shard_map/all_gather | solution.py:19
  8.7 600.1 %copy-start.7 = (bf16[16,8,16,256]{3,2,1,0:T(8,128)(2,1)}, bf16[16,8,16,256]{3,2,1,0:T(8,128)(2,1)S(1)}, u32[]{:S(2)}) copy-start(bf16[16,8,16,256]{3,2,1,0:T(8,128)(2,1)S(1)} %copy.150) | copy-start | bytes 3145732
  9.1 3.8 copy-start.26
  12.9 2.6 copy-start.12
  15.6 387.8 %all-gather.15.cloned.1.call-start = ((), (), s32[]{:S(2)}) async-start(), calls=%async_computation.3 | async-start | bytes 17825792 | tf_op jit(solution)/shard_map/all_gather | solution.py:19
  16.3 580.3 %all-gather.25.cloned.1.call-start = ((), (), s32[]{:S(2)}) async-start(), calls=%async_computation.10 | async-start | bytes 17825792 | tf_op jit(solution)/shard_map/all_gather | solution.py:49
  210.3 3.8 copy-start.34
  210.3 398.5 %copy-start.1 = (f32[16,256,128]{2,1,0:T(8,128)}, f32[16,256,128]{2,1,0:T(8,128)S(1)}, u32[]{:S(2)}) copy-start(f32[16,256,128]{2,1,0:T(8,128)S(1)} %get-tuple-element.852) | copy-start | bytes 6291460
  210.3 3.8 copy-start.30
  214.1 447.1 %all-gather.21.cloned.1.call-start = ((), (), s32[]{:S(2)}) async-start(), calls=%async_computation.6 | async-start | bytes 2228224 | tf_op jit(solution)/shard_map/all_gather | solution.py:281
  215.0 510.8 %all-gather.23.cloned.1.call-start = ((), (), s32[]{:S(2)}) async-start(), calls=%async_computation.7 | async-start | bytes 2228224 | tf_op jit(solution)/shard_map/all_gather | solution.py:282
  216.7 702.2 %all-gather.19.cloned.1.call-start = ((), (), s32[]{:S(2)}) async-start(), calls=%async_computation.5 | async-start | bytes 17825792 | tf_op jit(solution)/shard_map/all_gather | solution.py:19
  216.8 188.2 %copy-start.31 = (pred[64,64]{1,0:T(8,128)(4,1)}, pred[64,64]{1,0:T(8,128)(4,1)S(1)}, u32[]{:S(2)}) copy-start(pred[64,64]{1,0:T(8,128)(4,1)S(1)} %iota_compare_fusion) | copy-start | bytes 12292
  216.8 188.1 %copy-start.24 = (f32[2,16,64]{2,1,0:T(8,128)}, f32[2,16,64]{2,1,0:T(8,128)S(1)}, u32[]{:S(2)}) copy-start(f32[2,16,64]{2,1,0:T(8,128)S(1)} %copy.79) | copy-start | bytes 24580
  284.9 344.9 %copy-start.28 = (f32[2,64,16]{1,2,0:T(8,128)}, f32[2,64,16]{1,2,0:T(8,128)S(1)}, u32[]{:S(2)}) copy-start(f32[2,64,16]{1,2,0:T(8,128)S(1)} %copy.82) | copy-start | bytes 24580
  460.1 146.4 %copy-start.35 = (bf16[16,16]{1,0:T(8,128)(2,1)}, bf16[16,16]{1,0:T(8,128)(2,1)S(1)}, u32[]{:S(2)}) copy-start(bf16[16,16]{1,0:T(8,128)(2,1)S(1)} %get-tuple-element.1601) | copy-start | bytes 1540
  606.5 2.6 copy-start.15
  606.5 2.6 copy-start.36
  608.8 3.5 copy-start.9
  613.5 1.7 copy-start.14
  615.2 3.2 copy-start.33
  635.5 2.7 copy-start.11
  635.5 2.8 copy-start.17
  638.2 361.7 %reduce-scatter.3.cloned.1.call-start = ((), (), s32[]{:S(2)}) async-start(), calls=%async_computation.8 | async-start | bytes 2228224 | tf_op jit(solution)/shard_map/reduce_scatter | solution.py:335
  638.6 1.6 copy-start.13
  767.6 1.5 copy-start.19
  800.4 1.5 copy-start.19
  835.8 244.3 %reduce-scatter.5.cloned.1.call-start = ((), (), s32[]{:S(2)}) async-start(), calls=%async_computation.9 | async-start | bytes 2228224 | tf_op jit(solution)/shard_map/reduce_scatter | solution.py:338
  839.6 432.7 %all-gather.17.cloned.1.call-start = ((), (), s32[]{:S(2)}) async-start(), calls=%async_computation.4 | async-start | bytes 17825792 | tf_op jit(solution)/shard_map/all_gather | solution.py:19
  840.4 624.4 %all-gather.27.cloned.1.call-start = ((), (), s32[]{:S(2)}) async-start(), calls=%async_computation.11 | async-start | bytes 17825792 | tf_op jit(solution)/shard_map/all_gather | solution.py:49
  921.1 3.8 copy-start.16
  924.8 572.5 %all-reduce.3.cloned.1.call-start = ((), (), s32[]{:S(2)}) async-start(), calls=%async_computation.12 | async-start | bytes 131072 | tf_op jit(solution)/shard_map/psum | solution.py:145
  926.4 155.3 %copy-start.2 = (f32[16,256,128]{2,1,0:T(8,128)S(1)}, f32[16,256,128]{2,1,0:T(8,128)}, u32[]{:S(2)}) copy-start(f32[16,256,128]{2,1,0:T(8,128)} %copy-done.1) | copy-start | bytes 6291460
  926.4 155.2 %copy-start.29 = (f32[2,64,16]{1,2,0:T(8,128)S(1)}, f32[2,64,16]{1,2,0:T(8,128)}, u32[]{:S(2)}) copy-start(f32[2,64,16]{1,2,0:T(8,128)} %copy-done.28) | copy-start | bytes 24580
  1081.6 6.1 copy-start.6
  1081.6 6.1 copy-start.8
  1081.6 6.2 copy-start.25
  1081.6 6.1 copy-start.32
  1087.8 2.6 copy-start.23
  1087.8 3.4 copy-start.21
  1312.6 162.0 %copy-start.4 = (f32[16,256,128]{2,1,0:T(8,128)}, f32[16,256,128]{2,1,0:T(8,128)S(1)}, u32[]{:S(2)}) copy-start(f32[16,256,128]{2,1,0:T(8,128)S(1)} %get-tuple-element.857) | copy-start | bytes 6291460
  1474.7 2.5 copy-start.3
  1474.7 2.5 copy-start.27
  1477.0 3.3 copy-start.10
  1477.2 4.0 copy-start.37
  (4 other events, 3.9 us)
Sparse Core Ops, SparseCore 0:
  15.7 194.3 all-gather.12
  213.4 189.9 all-gather.14
  406.7 189.7 all-gather.24
  599.7 61.4 all-gather.20
  664.3 61.4 all-gather.22
  729.0 189.8 all-gather.18
  921.2 78.6 reduce-scatter.2
  1002.2 77.8 reduce-scatter.4
  1083.4 188.8 all-gather.16
  1274.9 189.7 all-gather.26
  1481.3 15.9 all-reduce.2
